TPU v7x, 32 devices: a whole 2x2x4 slice. The times are simulated.
32 devices in a mesh: groups: 2 (over y), patch: 8 (over z, x), head: 2 (over core).
Axes of the slice: x: 2, y: 2, z: 4, core: 2. Of those that a mesh axis runs over, the one named last changes fastest.
Arguments:
- queries: bfloat16 [2, 256, 1536], P(None, ('groups', 'patch'), 'head'), parts along dimension 1, may hold values from -15 to 15
- stale_pairs: bfloat16 [2, 320, 1536], P(None, ('groups', 'patch'), 'head'), parts along dimension 1, may hold values from -6 to 6
- step_pairs: bfloat16 [2, 2, 320, 1536], P(None, None, ('groups', 'patch'), 'head'), parts along dimension 2, may hold values from -6 to 6
- hidden: bfloat16 [256, 3072], P(('groups', 'patch'), 'head'), parts along dimension 0, may hold values from -3 to 3
- out_weight: bfloat16 [1536, 3072], P('head'), may hold values from -0.15625 to 0.15625
- gate_table: bfloat16 [28, 3072], replicated, may hold values from -4 to 4
- t_index: int32 [4], P('groups'), parts along dimension 0, may hold values from 0 to 27
- text_len: int32 [2], P('groups'), parts along dimension 0, may hold values from 1 to 32
Outputs:
- final_latents: bfloat16 [256, 3072], P(('groups', 'patch', 'head')), parts along dimension 0
There are 2 independent parts, one for each index of `groups`. A program takes and returns all parts, laid end to end along the dimension named above; an argument that names none is the same for every part. Nothing has to cross between parts.
All inputs are finite; a program needn't handle non-finite values.
Results may differ from a plain program's by a relative error of at most 0.0065.
Values may be sent and summed in bfloat16 or wider, within the bound.
A program may use at most 128 MiB of HBM per device.

v0:
```python
import jax
import jax.numpy as jnp
from jax import lax
from jax.sharding import PartitionSpec as P

HDIM = 128


def attend(query_rows, key_rows, value_rows, usable):
    count = query_rows.shape[0]
    total = key_rows.shape[0]
    heads_here = query_rows.shape[1] // HDIM
    qs = query_rows.reshape(count, heads_here, HDIM)
    ks = key_rows.reshape(total, heads_here, HDIM)
    vs = value_rows.reshape(total, heads_here, HDIM)
    scores = jnp.einsum("qhd,khd->hqk", qs, ks, preferred_element_type=jnp.float32) * (
        1.0 / HDIM**0.5
    )
    scores = jnp.where(usable[None, None, :], scores, jnp.float32(-1e30))
    top = jnp.max(scores, axis=2, keepdims=True)
    expo = jnp.exp(scores - top)
    weights = (expo / jnp.sum(expo, axis=2, keepdims=True)).astype(jnp.bfloat16)
    mixed = jnp.einsum("hqk,khd->qhd", weights, vs, preferred_element_type=jnp.float32)
    return mixed.reshape(count, heads_here * HDIM).astype(jnp.bfloat16)


def per_device(queries, stale_pairs, step_pairs, hidden, out_weight, gate_table, t_index, text_len):
    strip_rows = stale_pairs.shape[1]
    lat_rows = queries.shape[1]
    text_rows = strip_rows - lat_rows
    strip_count = lax.axis_size("patch")
    strip_index = lax.axis_index("patch")
    head_index = lax.axis_index("head")
    head_count = lax.axis_size("head")
    total = strip_rows * strip_count
    positions = jnp.arange(total, dtype=jnp.int32)
    within = positions % strip_rows
    holder = positions // strip_rows
    usable = (within < lat_rows) | (holder * text_rows + within - lat_rows < text_len[0])
    old_sets = lax.all_gather(stale_pairs, "patch", axis=1, tiled=True)
    first_sets = lax.all_gather(step_pairs[0], "patch", axis=1, tiled=True)
    remote_sets = (old_sets, first_sets)
    model_width = out_weight.shape[1]
    col_width = model_width // head_count

    def project(section):
        pairs = lax.dynamic_update_slice_in_dim(
            remote_sets[section], step_pairs[section], strip_index * strip_rows, axis=1
        )
        attended = attend(queries[section], pairs[0], pairs[1], usable)
        return jnp.dot(attended, out_weight, preferred_element_type=jnp.float32)

    state = hidden.astype(jnp.float32)
    first_proj = lax.psum_scatter(
        project(0).astype(jnp.bfloat16), "head", scatter_dimension=1, tiled=True
    ).astype(jnp.float32)
    gate_row = gate_table[t_index[0]].astype(jnp.float32)
    state = (
        state
        + lax.dynamic_slice_in_dim(gate_row, head_index * col_width, col_width, 0)[None, :]
        * first_proj
    )
    moved = lax.all_to_all(state, "head", split_axis=0, concat_axis=1, tiled=True)
    last_proj = lax.psum_scatter(project(1), "head", scatter_dimension=0, tiled=True)
    gate_full = gate_table[t_index[1]].astype(jnp.float32)
    return (moved + gate_full[None, :] * last_proj).astype(jnp.bfloat16)


def solution(mesh):
    return jax.shard_map(
        per_device,
        mesh=mesh,
        in_specs=(
            P(None, ("groups", "patch"), "head"),
            P(None, ("groups", "patch"), "head"),
            P(None, None, ("groups", "patch"), "head"),
            P(("groups", "patch"), "head"),
            P("head", None),
            P(),
            P("groups"),
            P("groups"),
        ),
        out_specs=P(("groups", "patch", "head"), None),
        check_vma=False,
    )
```

profile of v0, /device:TPU:0, one launch (start us, length us, event | category | flops | bytes accessed | tf_op | source)
XLA Modules:
  0.0 112.2 jit_solution(2523433137556579357)
XLA Ops:
  6.5 0.0 reduce-scatter.3.cloned.1.call-start
  6.5 0.9 slice_bitcast_fusion
  7.4 33.0 %all-gather = bf16[1,2,160,768]{3,1,0,2:T(2,128)(2,1)S(1)} all-gather(bf16[1,2,20,768]{3,1,0,2:T(2,128)(2,1)S(1)} %slice_bitcast_fusion), channel_id=2, replica_groups=mesh['groups'=2,'patch'=8,'head'=2] {'patch'}, dimensions={2}, use_global_device_ids=true | all-gather | bytes 552960 | tf_op jit(solution)/shard_map/all_gather | solution.py:41
  40.4 31.4 %all_gather.6 = bf16[2,160,768]{2,0,1:T(2,128)(2,1)S(1)} all-gather(bf16[2,20,768]{2,0,1:T(2,128)(2,1)} %param.9), channel_id=1, replica_groups=mesh['groups'=2,'patch'=8,'head'=2] {'patch'}, dimensions={1}, use_global_device_ids=true | all-gather | bytes 552960 | tf_op jit(solution)/shard_map/all_gather | solution.py:40
  71.7 0.8 fusion.33
  72.5 0.1 reshape_squeeze.20
  73.2 1.0 bitcast_dynamic-update-slice_fusion
  74.2 5.2 %slice_reduce_fusion.1 = (bf16[160,768]{1,0:T(8,128)(2,1)S(1)}, bf16[160,768]{1,0:T(8,128)(2,1)S(1)}, bf16[160,768]{1,0:T(8,128)(2,1)S(1)}, bf16[160,768]{1,0:T(8,128)(2,1)S(1)}) fusion(bf16[2,160,768]{2,0,1:T(2,128)(2,1)S(1)} %get-tuple-element.9, bf16[2,160,768]{2,0,1:T(2,128)(2,1)S(1)} %get-tuple-element.10), kind=kLoop, calls=%fused_computation.18 | loop fusion | bytes 1966080 | tf_op jit(solution)/shard_map/slice | solution.py:50
  79.3 0.4 fusion.35
  79.8 0.2 fusion.10
  80.0 0.0 copy-start.1
  80.0 0.0 copy-start
  80.0 3.7 %convolution_convert_fusion = bf16[16,3072]{1,0:T(8,128)(2,1)} fusion(bf16[768,3072]{1,0:T(8,128)(2,1)} %param.12, bf16[6,2,8,128]{3,2,1,0:T(8,128)(2,1)S(1)} %fusion.10), kind=kOutput, calls=%fused_computation.2 | convolution fusion | flops 75546624 | bytes 4841472 | tf_op jit(solution)/shard_map/dot_general | solution.py:51
  83.7 0.0 reduce-scatter.3.cloned.1.call-update
  83.8 0.0 reduce-scatter.5.cloned.1.call-start
  83.8 0.1 reshape_squeeze.23
  83.9 0.4 fusion.36
  84.3 0.2 fusion.11
  84.5 3.7 %fusion.22 = f32[16,3072]{1,0:T(8,128)} fusion(bf16[768,3072]{1,0:T(8,128)(2,1)} %param.12, bf16[6,2,8,128]{3,2,1,0:T(8,128)(2,1)S(1)} %fusion.11), kind=kOutput, calls=%fused_computation.38 | convolution fusion | flops 75497472 | bytes 4939776 | tf_op jit(solution)/shard_map/dot_general | solution.py:51
  88.3 0.0 reduce-scatter.5.cloned.1.call-update
  88.3 0.0 copy-done.1
  88.3 0.6 fusion.34
  92.5 0.8 dynamic-slice_convert_fusion
  93.4 0.8 fusion.29
  94.2 0.0 reduce-scatter.3.cloned.1.call-done
  94.2 0.0 copy-done
  94.2 0.8 add_bitcast_fusion
  95.1 3.8 %all_to_all.19 = f32[2,8,1536]{2,1,0:T(8,128)S(1)} all-to-all(f32[2,8,1536]{2,1,0:T(8,128)S(1)} %add_bitcast_fusion), channel_id=1, replica_groups=mesh['groups'=2,'patch'=8,'head'=2] {'head'}, dimensions={0} | all-to-all | bytes 196608 | tf_op jit(solution)/shard_map/all_to_all | solution.py:63
  98.9 5.0 %reduce-scatter.5.cloned.1.call-done = f32[8,3072]{1,0:T(8,128)} async-done(((f32[16,3072]{1,0:T(8,128)}), f32[8,3072]{1,0:T(8,128)}) %reduce-scatter.5.cloned.1.call-update) | async-done | bytes 98320 | tf_op jit(solution)/shard_map/reduce_scatter | solution.py:64
  103.8 1.5 %add_convert_fusion = bf16[8,3072]{1,0:T(8,128)(2,1)} fusion(f32[8,3072]{1,0:T(8,128)S(1)} %bitcast.74, f32[8,3072]{1,0:T(8,128)} %reduce-scatter.5.cloned.1.call-done, f32[3072]{0:T(1024)S(1)} %bitcast.75), kind=kLoop, calls=%fused_computation.29 | loop fusion | flops 73728 | bytes 258048 | tf_op jit(solution)/shard_map/convert_element_type | solution.py:66
  (1 shorter events, 0.0 us)
Async XLA Ops:
  6.5 87.7 %reduce-scatter.3.cloned.1.call-start = ((), (), s32[]{:S(2)}) async-start(), calls=%async_computation.3 | async-start | bytes 147456 | tf_op jit(solution)/shard_map/reduce_scatter | solution.py:54
  80.0 8.3 %copy-start.1 = (s32[2]{0:T(128)S(1)}, s32[2]{0:T(128)}, u32[]{:S(2)}) copy-start(s32[2]{0:T(128)} %param.14) | copy-start | bytes 28
  80.0 14.2 %copy-start = (bf16[16,1536]{1,0:T(8,128)(2,1)S(1)}, bf16[16,1536]{1,0:T(8,128)(2,1)}, u32[]{:S(2)}) copy-start(bf16[16,1536]{1,0:T(8,128)(2,1)} %param.11) | copy-start | bytes 147460
  83.8 20.1 %reduce-scatter.5.cloned.1.call-start = ((), (), s32[]{:S(2)}) async-start(), calls=%async_computation.4 | async-start | bytes 294912 | tf_op jit(solution)/shard_map/reduce_scatter | solution.py:64
Sparse Core Ops, SparseCore 0:
  83.9 8.8 reduce-scatter.2
  95.1 8.7 reduce-scatter.4
where the time goes:
time: 113 us; the launch traced here: 112 us
  blocking collectives  68.1 us (60%)
  between operations  17.8 us (16%)
  matrix products  8.77 us (8%)
  local copies, waits for them, and re-layouts  8.44 us (7%)
  waiting for transfers between devices  5.03 us (4%)
  other arithmetic  4.01 us (4%)
    all_gather x1, blocking collectives, per_device(): first_sets = lax.all_gather(step_pairs[0], 'patch', axis=1, tiled=True)  33 us
    all_gather x1, blocking collectives, per_device(): old_sets = lax.all_gather(stale_pairs, 'patch', axis=1, tiled=True)  31.4 us
    dot_general x2, matrix products, project(): return jnp.dot(attended, out_weight, preferred_element_type=jnp.float32)  7.5 us
    slice x2, local copies, waits for them, and re-layouts, project(): attended = attend(queries[section], pairs[0], pairs[1], usable)  5.91 us
    reduce_scatter x1, waiting for transfers between devices, per_device(): lax.psum_scatter(project(1), 'head', scatter_dimension=0, tiled=True)  4.98 us
    all_to_all x1, blocking collectives, per_device(): lax.all_to_all(state, 'head', split_axis=0, concat_axis=1, tiled=True)  3.79 us
  transfers between devices with their start and end apart: 2, of which 1 were waited for; matrix products, arithmetic and copies ran while one was open for 7% of the time, Pallas kernels for 0%

commit v1 on v0

v1 whole, which is shorter than its diff:
```python
import functools

import jax
import jax.numpy as jnp
from jax import lax
from jax.experimental import pallas as pl
from jax.experimental.pallas import tpu as pltpu
from jax.sharding import PartitionSpec as P

HDIM = 128
PAD = 32
MESH_ID = pl.DeviceIdType.MESH


def minor_extent(mesh):
    names = list(mesh.axis_names)
    order = [names.index("patch")] + [i for i, name in enumerate(names) if name != "patch"]
    line = mesh.devices.transpose(order).reshape(mesh.shape["patch"], -1)[:, 0]
    count = len(line)
    try:
        spots = [tuple(device.coords) for device in line]
    except AttributeError:
        return 2 if count % 2 == 0 else 1
    varying = lambda spot: [i for i in range(len(spot)) if spot[i] != spots[0][i]]
    extent = 1
    while extent < count and varying(spots[extent]) == varying(spots[1]) and len(varying(spots[1])) == 1:
        extent += 1
    return extent if count % extent == 0 else 1


def kernel(
    major, minor, heads_split,
    t_ref, len_ref, q_hbm, stale_hbm, step_hbm, hid_hbm, w_hbm, gate_hbm,
    out_ref,
    slots, padded, w_v, q_v, hid_v, gate_v, mixed, partial, arrived,
    load_sem, send_sem, recv_sem, swap_send, swap_recv,
):
    count = major * minor
    me = lax.axis_index("patch")
    mine = lax.axis_index("head")
    a, b = me // minor, me % minor
    strip_rows = stale_hbm.shape[1]
    lat_rows = q_hbm.shape[1]
    text_rows = strip_rows - lat_rows
    feats = q_hbm.shape[2]
    width = w_hbm.shape[1]
    col_width = hid_hbm.shape[1]
    out_rows = lat_rows // heads_split
    sides = (
        (a > 0, me - minor), (a < major - 1, me + minor),
        (b > 0, me - 1), (b < minor - 1, me + 1),
    )
    if minor == 1:
        sides = sides[:2]

    loads = [
        pltpu.make_async_copy(step_hbm.at[0], slots.at[me, 0], load_sem.at[0]),
        pltpu.make_async_copy(step_hbm.at[1], slots.at[me, 1], load_sem.at[1]),
        pltpu.make_async_copy(q_hbm, q_v, load_sem.at[2]),
        pltpu.make_async_copy(hid_hbm, hid_v, load_sem.at[3]),
        pltpu.make_async_copy(gate_hbm, gate_v, load_sem.at[4]),
        pltpu.make_async_copy(w_hbm, w_v, load_sem.at[5]),
    ]
    barrier = pltpu.get_barrier_semaphore()
    greeted = heads_split - 1
    for there, index in sides:
        greeted = greeted + there.astype(jnp.int32)

        @pl.when(there)
        def _():
            pl.semaphore_signal(barrier, inc=1, device_id={"patch": index}, device_id_type=MESH_ID)

    for k in range(1, heads_split):
        pl.semaphore_signal(
            barrier, inc=1, device_id={"head": (mine + k) % heads_split}, device_id_type=MESH_ID
        )
    for load in loads:
        load.start()
    pl.semaphore_wait(barrier, greeted)

    def remote(source, block, piece, side):
        return pltpu.make_async_remote_copy(
            src_ref=source,
            dst_ref=slots.at[block, piece],
            send_sem=send_sem.at[block, piece, side],
            recv_sem=recv_sem.at[block, piece],
            device_id={"patch": sides[side][1]},
            device_id_type=MESH_ID,
        )

    def spread(source, block, piece, to):
        for side in to:
            if side < len(sides):
                @pl.when(sides[side][0])
                def _():
                    remote(source, block, piece, side).start()

    def drain(block, piece, to):
        for side in to:
            if side < len(sides):
                @pl.when(sides[side][0])
                def _():
                    remote(slots.at[block, piece], block, piece, side).wait_send()

    def landed(block, piece):
        remote(slots.at[block, piece], block, piece, 0).wait_recv()

    own_source = (stale_hbm, step_hbm.at[0])
    for piece in range(2):
        spread(own_source[piece], me, piece, (0, 1, 2, 3))

    padded[...] = jnp.zeros_like(padded)
    loads[4].wait()
    plan_rows = lax.broadcasted_iota(jnp.int32, gate_v.shape, 0)
    table = gate_v[...].astype(jnp.float32)
    gates = [
        jnp.sum(jnp.where(plan_rows == t_ref[s], table, 0.0), axis=0, keepdims=True)
        for s in range(2)
    ]

    for t in range(1, major):
        for piece in range(2):
            for away, onward in ((a - t, 1), (a + t, 0)):
                @pl.when((away >= 0) & (away < major))
                def _():
                    block = away * minor + b
                    landed(block, piece)
                    spread(slots.at[block, piece], block, piece, (onward, 2, 3))

    for u in range(1, minor):
        for away, onward in ((b - u, 3), (b + u, 2)):
            @pl.when((away >= 0) & (away < minor))
            def _():
                def one(r, carry):
                    block = r * minor + away
                    for piece in range(2):
                        landed(block, piece)
                        if u < minor - 1:
                            spread(slots.at[block, piece], block, piece, (onward,))
                    return carry

                lax.fori_loop(0, major, one, 0)

    for load in (loads[0], loads[1], loads[2]):
        load.wait()

    keys = count * PAD
    place = lax.broadcasted_iota(jnp.int32, (1, keys), 1)
    holder, within = place // PAD, place % PAD
    usable = (within < lat_rows) | (
        (within < strip_rows) & (holder * text_rows + within - lat_rows < len_ref[0])
    )

    def attend(s):
        def fill(p, carry):
            start = pl.multiple_of(p * PAD, PAD)
            for kind in range(2):
                padded[kind, pl.ds(start, strip_rows), :] = slots[p, s, kind]
            return carry

        if count <= 8:
            for p in range(count):
                fill(p, 0)
        else:
            lax.fori_loop(0, count, fill, 0)
        for h in range(feats // HDIM):
            cols = slice(h * HDIM, (h + 1) * HDIM)
            scores = lax.dot_general(
                q_v[s, :, cols], padded[0, :, cols], (((1,), (1,)), ((), ())),
                preferred_element_type=jnp.float32,
            ) * (1.0 / HDIM**0.5)
            scores = jnp.where(usable, scores, jnp.float32(-1e30))
            top = jnp.max(scores, axis=1, keepdims=True)
            expo = jnp.exp(scores - top)
            weights = (expo * (1.0 / jnp.sum(expo, axis=1, keepdims=True))).astype(jnp.bfloat16)
            mixed[s, :, cols] = jnp.dot(
                weights, padded[1, :, cols], preferred_element_type=jnp.float32
            ).astype(jnp.bfloat16)

    chunks = 2 * heads_split
    chunk = width // chunks
    swaps = []
    for s in range(2):
        attend(s)
        if s == 0:
            loads[3].wait()
            loads[5].wait()
        for c in range(chunks):
            cols = slice(c * chunk, (c + 1) * chunk)
            term = gates[s][:, cols] * jnp.dot(
                mixed[s], w_v[:, cols], preferred_element_type=jnp.float32
            )
            if s == 0:
                owner, inner = (c * chunk) // col_width, (c * chunk) % col_width
                base = hid_v[:, inner:inner + chunk].astype(jnp.float32)
                partial[:, cols] = jnp.where(mine == owner, base, 0.0) + term
            else:
                partial[:, cols] = partial[:, cols] + term
                for k in range(1, heads_split):
                    peer = (mine + k) % heads_split
                    swap = pltpu.make_async_remote_copy(
                        src_ref=partial.at[pl.ds(pl.multiple_of(peer * out_rows, out_rows), out_rows), pl.ds(c * chunk, chunk)],
                        dst_ref=arrived.at[k - 1, :, pl.ds(c * chunk, chunk)],
                        send_sem=swap_send.at[k - 1, c],
                        recv_sem=swap_recv.at[k - 1, c],
                        device_id={"head": peer},
                        device_id_type=MESH_ID,
                    )
                    swap.start()
                    swaps.append((c, k, swap))

    own = pl.ds(pl.multiple_of(mine * out_rows, out_rows), out_rows)
    for c in range(chunks):
        cols = slice(c * chunk, (c + 1) * chunk)
        total = partial[own, cols]
        for cc, k, swap in swaps:
            if cc == c:
                swap.wait_recv()
                total = total + arrived[k - 1, :, cols]
        out_ref[:, cols] = total.astype(out_ref.dtype)

    for _, _, swap in swaps:
        swap.wait_send()
    for piece in range(2):
        drain(me, piece, (0, 1, 2, 3))
    for t in range(1, major):
        for piece in range(2):
            for away, onward in ((a - t, 1), (a + t, 0)):
                @pl.when((away >= 0) & (away < major))
                def _():
                    drain(away * minor + b, piece, (onward, 2, 3))
    for u in range(1, minor - 1):
        for away, onward in ((b - u, 3), (b + u, 2)):
            @pl.when((away >= 0) & (away < minor))
            def _():
                def one(r, carry):
                    for piece in range(2):
                        drain(r * minor + away, piece, (onward,))
                    return carry

                lax.fori_loop(0, major, one, 0)


def per_device(major, minor, heads_split, queries, stale_pairs, step_pairs, hidden, out_weight, gate_table, t_index, text_len):
    count = major * minor
    lat_rows, feats = queries.shape[1:]
    width = out_weight.shape[1]
    out_rows = lat_rows // heads_split
    chunks = 2 * heads_split
    anywhere = pl.BlockSpec(memory_space=pl.ANY)
    scalars = pl.BlockSpec(memory_space=pltpu.SMEM)
    return pl.pallas_call(
        functools.partial(kernel, major, minor, heads_split),
        out_shape=jax.ShapeDtypeStruct((out_rows, width), jnp.bfloat16),
        in_specs=[scalars] * 2 + [anywhere] * 6,
        out_specs=pl.BlockSpec(memory_space=pltpu.VMEM),
        scratch_shapes=[
            pltpu.VMEM((count,) + step_pairs.shape, jnp.bfloat16),
            pltpu.VMEM((2, count * PAD, feats), jnp.bfloat16),
            pltpu.VMEM(out_weight.shape, jnp.bfloat16),
            pltpu.VMEM(queries.shape, jnp.bfloat16),
            pltpu.VMEM(hidden.shape, jnp.bfloat16),
            pltpu.VMEM(gate_table.shape, jnp.bfloat16),
            pltpu.VMEM(queries.shape, jnp.bfloat16),
            pltpu.VMEM((lat_rows, width), jnp.float32),
            pltpu.VMEM((heads_split - 1, out_rows, width), jnp.float32),
            pltpu.SemaphoreType.DMA((6,)),
            pltpu.SemaphoreType.DMA((count, 2, 4)),
            pltpu.SemaphoreType.DMA((count, 2)),
            pltpu.SemaphoreType.DMA((heads_split - 1, chunks)),
            pltpu.SemaphoreType.DMA((heads_split - 1, chunks)),
        ],
        compiler_params=pltpu.CompilerParams(collective_id=0, has_side_effects=True),
        name="block",
    )(t_index, text_len, queries, stale_pairs, step_pairs, hidden, out_weight, gate_table)


def solution(mesh):
    minor = minor_extent(mesh)
    return jax.shard_map(
        functools.partial(per_device, mesh.shape["patch"] // minor, minor, mesh.shape["head"]),
        mesh=mesh,
        in_specs=(
            P(None, ("groups", "patch"), "head"),
            P(None, ("groups", "patch"), "head"),
            P(None, None, ("groups", "patch"), "head"),
            P(("groups", "patch"), "head"),
            P("head", None),
            P(),
            P("groups"),
            P("groups"),
        ),
        out_specs=P(("groups", "patch", "head"), None),
        check_vma=False,
    )
```

time: 113 us -> 34.4 us (0.30)
  blocking collectives: 68.1 us -> 0 us
  Pallas kernels: 0 us -> 29 us
  between operations: 17.8 us -> 0.66 us
  matrix products: 8.77 us -> 0 us
  waiting for transfers between devices: 5.03 us -> 0 us
  other arithmetic: 4.01 us -> 0 us
  local copies, waits for them, and re-layouts: 8.44 us -> 4.46 us
    all_gather x2 -> x0, blocking collectives: 64.3 us -> none  [the longest x1 33 us: per_device(): first_sets = lax.all_gather(step_pairs[0], 'patch', axis=1, tiled=True)]
    pallas_call x0 -> x1, Pallas kernels: none -> 29 us  [per_device(): pl.pallas_call(functools.partial(kernel, major, minor, heads_split), out_...]
    dot_general x4 -> x0, matrix products: 7.96 us -> none  [the longest x2 7.5 us: project(): return jnp.dot(attended, out_weight, preferred_element_type=jnp.float32)]
    slice x4 -> x0, local copies, waits for them, and re-layouts: 7.37 us -> none  [the longest x2 5.91 us: project(): attended = attend(queries[section], pairs[0], pairs[1], usable)]
    reduce_scatter x2 -> x0, waiting for transfers between devices: 5 us -> none  [the longest x1 4.98 us: per_device(): lax.psum_scatter(project(1), 'head', scatter_dimension=0, tiled=True)]
    unnamed x4 -> x3, local copies, waits for them, and re-layouts: 0.01 us -> 4.46 us
    all_to_all x1 -> x0, blocking collectives: 3.79 us -> none  [per_device(): lax.all_to_all(state, 'head', split_axis=0, concat_axis=1, tiled=True)]
    convert_element_type x1 -> x0, other arithmetic: 1.53 us -> none  [per_device(): return (moved + gate_full[None, :] * last_proj).astype(jnp.bfloat16)]
  transfers between devices with their start and end apart: 2 -> 0, of which waited for: 1 -> 0; matrix products, arithmetic and copies ran while one was open for 7% -> 0% of each run, Pallas kernels for 0% -> 0%
where the time goes in v1:
time: 34.4 us; the launch traced here: 34.1 us
  Pallas kernels  29 us (84%)
  local copies, waits for them, and re-layouts  4.46 us (13%)
  between operations  0.66 us (2%)
    pallas_call x1, Pallas kernels, per_device(): pl.pallas_call(functools.partial(kernel, major, minor, heads_split), out_...  29 us
    unnamed x3, local copies, waits for them, and re-layouts  4.46 us

profile of v1, /device:TPU:0, one launch (start us, length us, event | category | flops | bytes accessed | tf_op | source)
XLA Modules:
  0.0 34.1 jit_solution(10632269904662695148)
XLA Ops:
  0.7 1.5 %copy.9.stale_hbm = bf16[2,20,768]{2,1,0:T(8,128)(2,1)} copy(bf16[2,20,768]{2,0,1:T(2,128)(2,1)} %param.9) | data formatting | bytes 122880 | tf_op args[1]
  2.1 1.6 %copy.10.step_hbm = bf16[2,2,20,768]{3,2,1,0:T(8,128)(2,1)} copy(bf16[2,2,20,768]{3,1,2,0:T(2,128)(2,1)} %param.10) | data formatting | bytes 245760 | tf_op args[2]
  3.7 29.0 %block.1 = bf16[8,3072]{1,0:T(8,128)(2,1)} custom-call(s32[2]{0:T(128)} %t_ref.1, s32[1]{0:T(128)S(6)} %copy.12.len_ref, bf16[2,16,768]{2,1,0:T(8,128)(2,1)} %q_hbm.1, bf16[2,20,768]{2,1,0:T(8,128)(2,1)} %copy.9.stale_hbm, bf16[2,2,20,768]{3,2,1,0:T(8,128)(2,1)} %copy.10.step_hbm, bf16[16,1536]{1,0:T(8,128)(2,1)} %hid_hbm.1, bf16[768,3072]{1,0:T(8,128)(2,1)} %w_hbm.1, ...), custom_call_target="tpu_custom_call" | custom-call | tf_op jit(solution)/shard_map/block/pallas_call | solution.py:252
  32.7 1.4 %copy.13 = bf16[8,3072]{1,0:T(8,128)(2,1)} copy(bf16[8,3072]{1,0:T(8,128)(2,1)} %block.1) | data formatting | bytes 98304

commit v2 on v1

--- a/solution.py
+++ b/solution.py
@@ -32,14 +32,14 @@
     major, minor, heads_split,
     t_ref, len_ref, q_hbm, stale_hbm, step_hbm, hid_hbm, w_hbm, gate_hbm,
     out_ref,
-    slots, padded, w_v, q_v, hid_v, gate_v, mixed, partial, arrived,
+    slots, own_v, padded, w_v, q_v, hid_v, gate_v, partial, arrived,
     load_sem, send_sem, recv_sem, swap_send, swap_recv,
 ):
     count = major * minor
     me = lax.axis_index("patch")
     mine = lax.axis_index("head")
     a, b = me // minor, me % minor
-    strip_rows = stale_hbm.shape[1]
+    strip_rows = stale_hbm.shape[0]
     lat_rows = q_hbm.shape[1]
     text_rows = strip_rows - lat_rows
     feats = q_hbm.shape[2]
@@ -54,12 +54,11 @@
         sides = sides[:2]
 
     loads = [
-        pltpu.make_async_copy(step_hbm.at[0], slots.at[me, 0], load_sem.at[0]),
-        pltpu.make_async_copy(step_hbm.at[1], slots.at[me, 1], load_sem.at[1]),
-        pltpu.make_async_copy(q_hbm, q_v, load_sem.at[2]),
-        pltpu.make_async_copy(hid_hbm, hid_v, load_sem.at[3]),
-        pltpu.make_async_copy(gate_hbm, gate_v, load_sem.at[4]),
-        pltpu.make_async_copy(w_hbm, w_v, load_sem.at[5]),
+        pltpu.make_async_copy(step_hbm, own_v, load_sem.at[0]),
+        pltpu.make_async_copy(q_hbm, q_v, load_sem.at[1]),
+        pltpu.make_async_copy(hid_hbm, hid_v, load_sem.at[2]),
+        pltpu.make_async_copy(gate_hbm, gate_v, load_sem.at[3]),
+        pltpu.make_async_copy(w_hbm, w_v, load_sem.at[4]),
     ]
     barrier = pltpu.get_barrier_semaphore()
     greeted = heads_split - 1
@@ -109,40 +108,77 @@
     for piece in range(2):
         spread(own_source[piece], me, piece, (0, 1, 2, 3))
 
-    padded[...] = jnp.zeros_like(padded)
-    loads[4].wait()
+    def clear(p, carry):
+        rows = pl.ds(pl.multiple_of(p * PAD, PAD), PAD)
+        for s in range(2):
+            for kind in range(2):
+                padded[s, kind, rows, :] = jnp.zeros((PAD, feats), jnp.bfloat16)
+        return carry
+
+    lax.fori_loop(0, count, clear, 0)
+
+    def fill(block, s, source):
+        rows = pl.ds(pl.multiple_of(block * PAD, PAD), strip_rows)
+        both = source[...]
+        for kind in range(2):
+            padded[s, kind, rows, :] = both[:, kind, :]
+
+    loads[3].wait()
     plan_rows = lax.broadcasted_iota(jnp.int32, gate_v.shape, 0)
     table = gate_v[...].astype(jnp.float32)
     gates = [
         jnp.sum(jnp.where(plan_rows == t_ref[s], table, 0.0), axis=0, keepdims=True)
         for s in range(2)
     ]
+    loads[0].wait()
+    for s in range(2):
+        fill(me, s, own_v.at[s])
+
+    def cross(t, piece):
+        for away in {0: (a,)}.get(t, (a - t, a + t)):
+            @pl.when((away >= 0) & (away < major))
+            def _():
+                block = away * minor + (1 - b)
+                landed(block, piece)
+                fill(block, piece, slots.at[block, piece])
 
     for t in range(1, major):
+        steps = ((a - t, 1), (a + t, 0))
         for piece in range(2):
-            for away, onward in ((a - t, 1), (a + t, 0)):
+            for away, onward in steps:
                 @pl.when((away >= 0) & (away < major))
                 def _():
                     block = away * minor + b
                     landed(block, piece)
                     spread(slots.at[block, piece], block, piece, (onward, 2, 3))
 
-    for u in range(1, minor):
-        for away, onward in ((b - u, 3), (b + u, 2)):
-            @pl.when((away >= 0) & (away < minor))
-            def _():
-                def one(r, carry):
-                    block = r * minor + away
-                    for piece in range(2):
-                        landed(block, piece)
-                        if u < minor - 1:
-                            spread(slots.at[block, piece], block, piece, (onward,))
-                    return carry
-
-                lax.fori_loop(0, major, one, 0)
-
-    for load in (loads[0], loads[1], loads[2]):
-        load.wait()
+        for piece in range(2):
+            for away, onward in steps:
+                @pl.when((away >= 0) & (away < major))
+                def _():
+                    block = away * minor + b
+                    fill(block, piece, slots.at[block, piece])
+
+            if minor == 2:
+                cross(t - 1, piece)
+
+    if minor > 2:
+        for u in range(1, minor):
+            for away, onward in ((b - u, 3), (b + u, 2)):
+                @pl.when((away >= 0) & (away < minor))
+                def _():
+                    def one(r, carry):
+                        block = r * minor + away
+                        for piece in range(2):
+                            landed(block, piece)
+                            if u < minor - 1:
+                                spread(slots.at[block, piece], block, piece, (onward,))
+                            fill(block, piece, slots.at[block, piece])
+                        return carry
+
+                    lax.fori_loop(0, major, one, 0)
+
+    loads[1].wait()
 
     keys = count * PAD
     place = lax.broadcasted_iota(jnp.int32, (1, keys), 1)
@@ -150,45 +186,46 @@
     usable = (within < lat_rows) | (
         (within < strip_rows) & (holder * text_rows + within - lat_rows < len_ref[0])
     )
+    heads = [slice(h * HDIM, (h + 1) * HDIM) for h in range(feats // HDIM)]
 
     def attend(s):
-        def fill(p, carry):
-            start = pl.multiple_of(p * PAD, PAD)
-            for kind in range(2):
-                padded[kind, pl.ds(start, strip_rows), :] = slots[p, s, kind]
-            return carry
-
-        if count <= 8:
-            for p in range(count):
-                fill(p, 0)
-        else:
-            lax.fori_loop(0, count, fill, 0)
-        for h in range(feats // HDIM):
-            cols = slice(h * HDIM, (h + 1) * HDIM)
-            scores = lax.dot_general(
-                q_v[s, :, cols], padded[0, :, cols], (((1,), (1,)), ((), ())),
+        scores = jnp.concatenate(
+            [
+                lax.dot_general(
+                    q_v[s, :, cols], padded[s, 0, :, cols], (((1,), (1,)), ((), ())),
+                    preferred_element_type=jnp.float32,
+                )
+                for cols in heads
+            ],
+            axis=0,
+        ) * (1.0 / HDIM**0.5)
+        scores = jnp.where(usable, scores, jnp.float32(-1e30))
+        top = jnp.max(scores, axis=1, keepdims=True)
+        expo = jnp.exp(scores - top)
+        weights = (expo * (1.0 / jnp.sum(expo, axis=1, keepdims=True))).astype(jnp.bfloat16)
+        parts = [
+            jnp.dot(
+                weights[h * lat_rows:(h + 1) * lat_rows], padded[s, 1, :, cols],
                 preferred_element_type=jnp.float32,
-            ) * (1.0 / HDIM**0.5)
-            scores = jnp.where(usable, scores, jnp.float32(-1e30))
-            top = jnp.max(scores, axis=1, keepdims=True)
-            expo = jnp.exp(scores - top)
-            weights = (expo * (1.0 / jnp.sum(expo, axis=1, keepdims=True))).astype(jnp.bfloat16)
-            mixed[s, :, cols] = jnp.dot(
-                weights, padded[1, :, cols], preferred_element_type=jnp.float32
             ).astype(jnp.bfloat16)
+            for h, cols in enumerate(heads)
+        ]
+        return jnp.concatenate(parts, axis=1)
 
     chunks = 2 * heads_split
     chunk = width // chunks
     swaps = []
     for s in range(2):
-        attend(s)
+        if minor == 2:
+            cross(major - 1, s)
+        mixed = attend(s)
         if s == 0:
-            loads[3].wait()
-            loads[5].wait()
+            loads[2].wait()
+            loads[4].wait()
         for c in range(chunks):
             cols = slice(c * chunk, (c + 1) * chunk)
             term = gates[s][:, cols] * jnp.dot(
-                mixed[s], w_v[:, cols], preferred_element_type=jnp.float32
+                mixed, w_v[:, cols], preferred_element_type=jnp.float32
             )
             if s == 0:
                 owner, inner = (c * chunk) // col_width, (c * chunk) % col_width
@@ -243,6 +280,8 @@
 
 def per_device(major, minor, heads_split, queries, stale_pairs, step_pairs, hidden, out_weight, gate_table, t_index, text_len):
     count = major * minor
+    stale_pairs = jnp.transpose(stale_pairs, (1, 0, 2))
+    step_pairs = jnp.transpose(step_pairs, (0, 2, 1, 3))
     lat_rows, feats = queries.shape[1:]
     width = out_weight.shape[1]
     out_rows = lat_rows // heads_split
@@ -256,15 +295,15 @@
         out_specs=pl.BlockSpec(memory_space=pltpu.VMEM),
         scratch_shapes=[
             pltpu.VMEM((count,) + step_pairs.shape, jnp.bfloat16),
-            pltpu.VMEM((2, count * PAD, feats), jnp.bfloat16),
+            pltpu.VMEM(step_pairs.shape, jnp.bfloat16),
+            pltpu.VMEM((2, 2, count * PAD, feats), jnp.bfloat16),
             pltpu.VMEM(out_weight.shape, jnp.bfloat16),
             pltpu.VMEM(queries.shape, jnp.bfloat16),
             pltpu.VMEM(hidden.shape, jnp.bfloat16),
             pltpu.VMEM(gate_table.shape, jnp.bfloat16),
-            pltpu.VMEM(queries.shape, jnp.bfloat16),
             pltpu.VMEM((lat_rows, width), jnp.float32),
             pltpu.VMEM((heads_split - 1, out_rows, width), jnp.float32),
-            pltpu.SemaphoreType.DMA((6,)),
+            pltpu.SemaphoreType.DMA((5,)),
             pltpu.SemaphoreType.DMA((count, 2, 4)),
             pltpu.SemaphoreType.DMA((count, 2)),
             pltpu.SemaphoreType.DMA((heads_split - 1, chunks)),

time: 34.4 us -> 26.4 us (0.77)
  Pallas kernels: 29 us -> 24.1 us
  local copies, waits for them, and re-layouts: 4.46 us -> 1.42 us
    pallas_call x1, Pallas kernels: 29 us -> 24.1 us  [per_device(): pl.pallas_call(functools.partial(kernel, major, minor, heads_split), out_...]
    unnamed x3 -> x1, local copies, waits for them, and re-layouts: 4.46 us -> 1.42 us
where the time goes in v2:
time: 26.4 us; the launch traced here: 26.2 us
  Pallas kernels  24.1 us (91%)
  local copies, waits for them, and re-layouts  1.42 us (5%)
  between operations  0.66 us (2%)
    pallas_call x1, Pallas kernels, per_device(): pl.pallas_call(functools.partial(kernel, major, minor, heads_split), out_...  24.1 us
    unnamed x1, local copies, waits for them, and re-layouts  1.42 us

profile of v2, /device:TPU:0, one launch (start us, length us, event | category | flops | bytes accessed | tf_op | source)
XLA Modules:
  0.0 26.2 jit_solution(1832822368511511903)
XLA Ops:
  0.7 24.1 %block.1 = bf16[8,3072]{1,0:T(8,128)(2,1)} custom-call(s32[2]{0:T(128)} %t_ref.1, s32[1]{0:T(128)S(6)} %copy.10.len_ref, bf16[2,16,768]{2,1,0:T(8,128)(2,1)} %q_hbm.1, bf16[20,2,768]{2,1,0:T(2,128)(2,1)} %bitcast.3, bf16[2,20,2,768]{3,2,1,0:T(2,128)(2,1)} %bitcast.2, bf16[16,1536]{1,0:T(8,128)(2,1)} %hid_hbm.1, bf16[768,3072]{1,0:T(8,128)(2,1)} %w_hbm.1, ...), custom_call_target="tpu_custom_call" | custom-call | tf_op jit(solution)/shard_map/block/pallas_call | solution.py:291
  24.8 1.4 %copy.11 = bf16[8,3072]{1,0:T(8,128)(2,1)} copy(bf16[8,3072]{1,0:T(8,128)(2,1)} %block.1) | data formatting | bytes 98304

commit v3 on v2

--- a/solution.py
+++ b/solution.py
@@ -212,7 +212,7 @@
         ]
         return jnp.concatenate(parts, axis=1)
 
-    chunks = 2 * heads_split
+    chunks = heads_split
     chunk = width // chunks
     swaps = []
     for s in range(2):
@@ -233,30 +233,27 @@
                 partial[:, cols] = jnp.where(mine == owner, base, 0.0) + term
             else:
                 partial[:, cols] = partial[:, cols] + term
-                for k in range(1, heads_split):
-                    peer = (mine + k) % heads_split
-                    swap = pltpu.make_async_remote_copy(
-                        src_ref=partial.at[pl.ds(pl.multiple_of(peer * out_rows, out_rows), out_rows), pl.ds(c * chunk, chunk)],
-                        dst_ref=arrived.at[k - 1, :, pl.ds(c * chunk, chunk)],
-                        send_sem=swap_send.at[k - 1, c],
-                        recv_sem=swap_recv.at[k - 1, c],
-                        device_id={"head": peer},
-                        device_id_type=MESH_ID,
-                    )
-                    swap.start()
-                    swaps.append((c, k, swap))
+    for k in range(1, heads_split):
+        peer = (mine + k) % heads_split
+        swap = pltpu.make_async_remote_copy(
+            src_ref=partial.at[pl.ds(pl.multiple_of(peer * out_rows, out_rows), out_rows)],
+            dst_ref=arrived.at[k - 1],
+            send_sem=swap_send.at[k - 1],
+            recv_sem=swap_recv.at[k - 1],
+            device_id={"head": peer},
+            device_id_type=MESH_ID,
+        )
+        swap.start()
+        swaps.append(swap)
 
     own = pl.ds(pl.multiple_of(mine * out_rows, out_rows), out_rows)
-    for c in range(chunks):
-        cols = slice(c * chunk, (c + 1) * chunk)
-        total = partial[own, cols]
-        for cc, k, swap in swaps:
-            if cc == c:
-                swap.wait_recv()
-                total = total + arrived[k - 1, :, cols]
-        out_ref[:, cols] = total.astype(out_ref.dtype)
-
-    for _, _, swap in swaps:
+    total = partial[own]
+    for k, swap in enumerate(swaps):
+        swap.wait_recv()
+        total = total + arrived[k]
+    out_ref[...] = total.astype(out_ref.dtype)
+
+    for swap in swaps:
         swap.wait_send()
     for piece in range(2):
         drain(me, piece, (0, 1, 2, 3))
@@ -285,7 +282,6 @@
     lat_rows, feats = queries.shape[1:]
     width = out_weight.shape[1]
     out_rows = lat_rows // heads_split
-    chunks = 2 * heads_split
     anywhere = pl.BlockSpec(memory_space=pl.ANY)
     scalars = pl.BlockSpec(memory_space=pltpu.SMEM)
     return pl.pallas_call(
@@ -306,8 +302,8 @@
             pltpu.SemaphoreType.DMA((5,)),
             pltpu.SemaphoreType.DMA((count, 2, 4)),
             pltpu.SemaphoreType.DMA((count, 2)),
-            pltpu.SemaphoreType.DMA((heads_split - 1, chunks)),
-            pltpu.SemaphoreType.DMA((heads_split - 1, chunks)),
+            pltpu.SemaphoreType.DMA((heads_split - 1,)),
+            pltpu.SemaphoreType.DMA((heads_split - 1,)),
         ],
         compiler_params=pltpu.CompilerParams(collective_id=0, has_side_effects=True),
         name="block",

time: 26.4 us -> 25.9 us (0.981)
  Pallas kernels: 24.1 us -> 23.6 us
    pallas_call x1, Pallas kernels: 24.1 us -> 23.6 us  [per_device(): pl.pallas_call(functools.partial(kernel, major, minor, heads_split), out_...]
where the time goes in v3:
time: 25.9 us; the launch traced here: 25.7 us
  Pallas kernels  23.6 us (91%)
  local copies, waits for them, and re-layouts  1.42 us (5%)
  between operations  0.66 us (3%)
    pallas_call x1, Pallas kernels, per_device(): pl.pallas_call(functools.partial(kernel, major, minor, heads_split), out_...  23.6 us
    unnamed x1, local copies, waits for them, and re-layouts  1.42 us

profile of v3, /device:TPU:0, one launch (start us, length us, event | category | flops | bytes accessed | tf_op | source)
XLA Modules:
  0.0 25.7 jit_solution(16717784961347422706)
XLA Ops:
  0.7 23.6 %block.1 = bf16[8,3072]{1,0:T(8,128)(2,1)} custom-call(s32[2]{0:T(128)} %t_ref.1, s32[1]{0:T(128)S(6)} %copy.10.len_ref, bf16[2,16,768]{2,1,0:T(8,128)(2,1)} %q_hbm.1, bf16[20,2,768]{2,1,0:T(2,128)(2,1)} %bitcast.3, bf16[2,20,2,768]{3,2,1,0:T(2,128)(2,1)} %bitcast.2, bf16[16,1536]{1,0:T(8,128)(2,1)} %hid_hbm.1, bf16[768,3072]{1,0:T(8,128)(2,1)} %w_hbm.1, ...), custom_call_target="tpu_custom_call" | custom-call | tf_op jit(solution)/shard_map/block/pallas_call | solution.py:287
  24.3 1.4 %copy.11 = bf16[8,3072]{1,0:T(8,128)(2,1)} copy(bf16[8,3072]{1,0:T(8,128)(2,1)} %block.1) | data formatting | bytes 98304
